TPU v7x, 512 devices: a whole 4x4x16 slice. The times are simulated.
512 devices in a mesh: grid: 32 (over x, y, core), band: 16 (over z).
Axes of the slice: x: 4, y: 4, z: 16, core: 2. Of those that a mesh axis runs over, the one named last changes fastest.
Arguments:
- orbitals: bfloat16 [32768, 512], P('grid', 'band'), may hold values from -6 to 6
- rotation: bfloat16 [512, 32768], P('grid', 'band'), may hold values from -0.25 to 0.25
Outputs:
- rotated: bfloat16 [32768, 32768], P('grid', 'band')
All inputs are finite; a program needn't handle non-finite values.
Results may differ from a plain program's by a relative error of at most 0.001.
Values may be sent and summed in bfloat16 or wider, within the bound.
No kernel may reach another device: no remote copies, remote signals or barrier semaphores. Data moves between devices by JAX's collectives and lax.ppermute only.
A program may use at most 64 MiB of HBM per device.

v0:
```python
import jax
import jax.numpy as jnp
from jax import lax
from jax.sharding import PartitionSpec as P

ALONE = 896


def spread(block, axis):
    n = lax.axis_size(axis)
    copies = jnp.broadcast_to(block[None], (n, *block.shape))
    return lax.all_to_all(copies, axis, 0, 0, tiled=True).reshape(-1, block.shape[1])


def on_device(orbitals, rotation):
    columns = orbitals.T
    all_rows = spread(rotation, "grid")
    rest = spread(columns[:, ALONE:], "band")
    main = lax.all_gather(columns[:, :ALONE], "band", axis=0, tiled=True)
    all_cols = jnp.concatenate([main, rest], axis=1)
    total = lax.dot_general(
        all_cols, all_rows, (((0,), (0,)), ((), ())), preferred_element_type=jnp.float32
    )
    return total.astype(jnp.bfloat16)


def solution(mesh):
    in_specs = (P("grid", "band"), P("grid", "band"))
    out_specs = P("grid", "band")
    return jax.shard_map(
        on_device, mesh=mesh, in_specs=in_specs, out_specs=out_specs, check_vma=False
    )
```

profile of v0, /device:TPU:2, one launch (start us, length us, event | category | flops | bytes accessed | tf_op | source)
XLA Modules:
  0.0 78.8 jit_solution(8730877428883429115)
XLA Ops:
  0.0 0.7 slice.9
  0.7 29.7 %all_to_all.10 = bf16[16,32,128]{2,1,0:T(8,128)(2,1)S(1)} all-to-all(bf16[16,32,128]{2,1,0:T(8,128)(2,1)S(1)} %broadcast_in_dim.4), channel_id=1, replica_groups=mesh['grid'=32,'band'=16] {'band'}, dimensions={0} | all-to-all | bytes 262144 | tf_op jit(solution)/shard_map/all_to_all | solution.py:12
  30.4 2.4 %broadcast_in_dim.5 = bf16[32,16,2048]{2,1,0:T(8,128)(2,1)} broadcast(bf16[16,2048]{1,0:T(8,128)(2,1)} %param.3), dimensions={1,2} | broadcast | bytes 2162688 | tf_op jit(solution)/shard_map/broadcast_in_dim | solution.py:11
  32.8 0.0 copy-start
  32.8 7.8 %all-to-all-start.1 = ((bf16[32,16,2048]{2,1,0:T(8,128)(2,1)}), bf16[32,16,2048]{2,1,0:T(8,128)(2,1)S(1)}, u32[]{:S(2)}, u32[]{:S(2)}) async-start(bf16[32,16,2048]{2,1,0:T(8,128)(2,1)} %broadcast_in_dim.5), calls=%async_computation.1 | async-start | bytes 4194304 | tf_op jit(solution)/shard_map/all_to_all | solution.py:12
  40.6 0.0 copy-done
  40.6 33.8 %all_gather.3 = bf16[512,896]{1,0:T(8,128)(2,1)S(1)} all-gather(bf16[32,896]{1,0:T(8,128)(2,1)S(1)} %slice.8), channel_id=1, replica_groups=mesh['grid'=32,'band'=16] {'band'}, dimensions={0}, use_global_device_ids=true | all-gather | bytes 974848 | tf_op jit(solution)/shard_map/all_gather | solution.py:19
  74.4 0.0 all-to-all-done.1
  74.4 4.4 %convolution_convert_fusion = bf16[1024,2048]{1,0:T(8,128)(2,1)} fusion(bf16[512,2048]{1,0:T(8,128)(2,1)S(1)} %bitcast.4, bf16[512,128]{1,0:T(8,128)(2,1)S(1)} %bitcast.5, bf16[512,896]{1,0:T(8,128)(2,1)S(1)} %all_gather.3), kind=kOutput, calls=%fused_computation | convolution fusion | flops 2151677952 | bytes 7340032 | tf_op jit(solution)/shard_map/dot_general | solution.py:21
  (2 shorter events, 0.0 us)
Async XLA Ops:
  32.8 7.8 %copy-start = (bf16[1024,32]{0,1:T(8,128)(2,1)S(1)}, bf16[1024,32]{0,1:T(8,128)(2,1)}, u32[]{:S(2)}) copy-start(bf16[1024,32]{0,1:T(8,128)(2,1)} %param.2) | copy-start | bytes 196612
  32.8 41.6 %all-to-all-start.1 = ((bf16[32,16,2048]{2,1,0:T(8,128)(2,1)}), bf16[32,16,2048]{2,1,0:T(8,128)(2,1)S(1)}, u32[]{:S(2)}, u32[]{:S(2)}) async-start(bf16[32,16,2048]{2,1,0:T(8,128)(2,1)} %broadcast_in_dim.5), calls=%async_computation.1 | async-start | bytes 4194304 | tf_op jit(solution)/shard_map/all_to_all | solution.py:12
where the time goes:
time: 79.2 us; the launch traced here: 78.8 us
  blocking collectives  63.5 us (80%)
  starting transfers between devices  7.76 us (10%)
  matrix products  4.39 us (6%)
  local copies, waits for them, and re-layouts  3.14 us (4%)
    all_gather x1, blocking collectives, on_device(): main = lax.all_gather(columns[:, :ALONE], 'band', axis=0, tiled=True)  33.8 us
    all_to_all x1, blocking collectives, spread(): lax.all_to_all(copies, axis, 0, 0, tiled=True).reshape(-1, block.shape[1])  29.7 us
    all_to_all x1, starting transfers between devices, spread(): lax.all_to_all(copies, axis, 0, 0, tiled=True).reshape(-1, block.shape[1])  7.76 us
    dot_general x1, matrix products, on_device(): lax.dot_general(all_cols, all_rows, (((0,), (0,)), ((), ())), preferred_e...  4.39 us
    broadcast_in_dim x2, local copies, waits for them, and re-layouts, spread(): copies = jnp.broadcast_to(block[None], (n, *block.shape))  2.43 us
  transfers between devices with their start and end apart: 1, of which 0 were waited for; matrix products, arithmetic and copies ran while one was open for 0% of the time, Pallas kernels for 0%

commit v1 on v0

--- a/solution.py
+++ b/solution.py
@@ -4,6 +4,15 @@
 from jax.sharding import PartitionSpec as P
 
 ALONE = 896
+
+
+def load_pages(xx):
+    return jnp.concatenate(
+        lax.all_to_all(
+            jnp.stack(lax.axis_size("band") * [xx]), axis_name="band", split_axis=0, concat_axis=0
+        ),
+        axis=0,
+    )
 
 
 def spread(block, axis):
@@ -16,7 +25,7 @@
     columns = orbitals.T
     all_rows = spread(rotation, "grid")
     rest = spread(columns[:, ALONE:], "band")
-    main = lax.all_gather(columns[:, :ALONE], "band", axis=0, tiled=True)
+    main = load_pages(columns[:, :ALONE])
     all_cols = jnp.concatenate([main, rest], axis=1)
     total = lax.dot_general(
         all_cols, all_rows, (((0,), (0,)), ((), ())), preferred_element_type=jnp.float32

time: 79.2 us -> 123 us (1.55)
  the two profiles are of different devices: /device:TPU:2 before, /device:TPU:4 now
where the time goes in v1:
time: 123 us; the launch traced here: 122 us
  blocking collectives  81 us (66%)
  waiting for transfers between devices  25.9 us (21%)
  starting transfers between devices  7.73 us (6%)
  matrix products  4.39 us (4%)
  local copies, waits for them, and re-layouts  3.21 us (3%)
    all_to_all x1, blocking collectives, load_pages(): lax.all_to_all(jnp.stack(lax.axis_size('band') * [xx]), axis_name='band',...  51.3 us
    all_to_all x1, blocking collectives, spread(): lax.all_to_all(copies, axis, 0, 0, tiled=True).reshape(-1, block.shape[1])  29.7 us
    all_to_all x1, waiting for transfers between devices, spread(): lax.all_to_all(copies, axis, 0, 0, tiled=True).reshape(-1, block.shape[1])  25.9 us
    all_to_all x1, starting transfers between devices, spread(): lax.all_to_all(copies, axis, 0, 0, tiled=True).reshape(-1, block.shape[1])  7.73 us
    dot_general x1, matrix products, on_device(): lax.dot_general(all_cols, all_rows, (((0,), (0,)), ((), ())), preferred_e...  4.39 us
  transfers between devices with their start and end apart: 1, of which 1 were waited for; matrix products, arithmetic and copies ran while one was open for 0% of the time, Pallas kernels for 0%

profile of v1, /device:TPU:4, one launch (start us, length us, event | category | flops | bytes accessed | tf_op | source)
XLA Modules:
  0.0 122.3 jit_solution(8781690993555527606)
XLA Ops:
  0.0 0.7 slice.9
  0.7 29.7 %all_to_all.15 = bf16[16,32,128]{2,1,0:T(8,128)(2,1)S(1)} all-to-all(bf16[16,32,128]{2,1,0:T(8,128)(2,1)S(1)} %broadcast_in_dim.4), channel_id=1, replica_groups=mesh['grid'=32,'band'=16] {'band'}, dimensions={0} | all-to-all | bytes 262144 | tf_op jit(solution)/shard_map/all_to_all | solution.py:21
  30.4 2.4 %broadcast_in_dim.5 = bf16[32,16,2048]{2,1,0:T(8,128)(2,1)} broadcast(bf16[16,2048]{1,0:T(8,128)(2,1)} %param.3), dimensions={1,2} | broadcast | bytes 2162688 | tf_op jit(solution)/shard_map/broadcast_in_dim | solution.py:20
  32.8 0.0 copy-start
  32.8 7.7 %all-to-all-start.2 = ((bf16[32,16,2048]{2,1,0:T(8,128)(2,1)}), bf16[32,16,2048]{2,1,0:T(8,128)(2,1)S(1)}, u32[]{:S(2)}, u32[]{:S(2)}) async-start(bf16[32,16,2048]{2,1,0:T(8,128)(2,1)} %broadcast_in_dim.5), calls=%async_computation.2 | async-start | bytes 4194304 | tf_op jit(solution)/shard_map/all_to_all | solution.py:21
  40.6 0.0 copy-done
  40.6 25.9 %all-to-all-done.2 = bf16[32,16,2048]{2,1,0:T(8,128)(2,1)S(1)} async-done(((bf16[32,16,2048]{2,1,0:T(8,128)(2,1)}), bf16[32,16,2048]{2,1,0:T(8,128)(2,1)S(1)}, u32[]{:S(2)}, u32[]{:S(2)}) %all-to-all-start.2) | async-done | bytes 2097184 | tf_op jit(solution)/shard_map/all_to_all | solution.py:21
  66.5 0.1 stack.2
  66.6 51.3 %all_to_all.16 = bf16[16,32,896]{2,1,0:T(8,128)(2,1)S(1)} all-to-all(bf16[16,32,896]{2,1,0:T(8,128)(2,1)S(1)} %stack.2), channel_id=1, replica_groups=mesh['grid'=32,'band'=16] {'band'}, dimensions={0} | all-to-all | bytes 1835008 | tf_op jit(solution)/shard_map/all_to_all | solution.py:11
  117.9 4.4 %convolution_convert_fusion = bf16[1024,2048]{1,0:T(8,128)(2,1)} fusion(bf16[512,2048]{1,0:T(8,128)(2,1)S(1)} %bitcast.5, bf16[512,128]{1,0:T(8,128)(2,1)S(1)} %bitcast.7, bf16[512,896]{1,0:T(8,128)(2,1)S(1)} %bitcast.6), kind=kOutput, calls=%fused_computation | convolution fusion | flops 2151677952 | bytes 7340032 | tf_op jit(solution)/shard_map/dot_general | solution.py:30
  (2 shorter events, 0.0 us)
Async XLA Ops:
  32.8 7.7 %copy-start = (bf16[1024,32]{0,1:T(8,128)(2,1)S(1)}, bf16[1024,32]{0,1:T(8,128)(2,1)}, u32[]{:S(2)}) copy-start(bf16[1024,32]{0,1:T(8,128)(2,1)} %param.2) | copy-start | bytes 196612
  32.8 33.7 %all-to-all-start.2 = ((bf16[32,16,2048]{2,1,0:T(8,128)(2,1)}), bf16[32,16,2048]{2,1,0:T(8,128)(2,1)S(1)}, u32[]{:S(2)}, u32[]{:S(2)}) async-start(bf16[32,16,2048]{2,1,0:T(8,128)(2,1)} %broadcast_in_dim.5), calls=%async_computation.2 | async-start | bytes 4194304 | tf_op jit(solution)/shard_map/all_to_all | solution.py:21
